TPU v7x, 32 devices: a whole 2x2x4 slice. The times are simulated.
32 devices in a mesh: seq: 8 (over z, x), head: 4 (over y, core).
Axes of the slice: x: 2, y: 2, z: 4, core: 2. Of those that a mesh axis runs over, the one named last changes fastest.
Arguments:
- hidden_states: bfloat16 [2, 352, 5120], P(None, 'seq', 'head'), may hold values from -60 to 60
- clean_states: bfloat16 [2, 352, 5120], P(None, 'seq', 'head'), may hold values from -60 to 60
- w_query: bfloat16 [5120, 2560], P(None, 'head'), may hold values from -2 to 2
- w_key: bfloat16 [5120, 2560], P(None, 'head'), may hold values from -2 to 2
- w_value: bfloat16 [5120, 2560], P(None, 'head'), may hold values from -0.078125 to 0.078125
- q_gain: float32 [2560], P('head'), may hold values from 0.1 to 1.9
- k_gain: float32 [2560], P('head'), may hold values from 0.1 to 1.9
- cache_keys: bfloat16 [9, 352, 2560], P(None, 'seq', 'head'), may hold values from -1300 to 1300
- cache_values: bfloat16 [9, 352, 2560], P(None, 'seq', 'head'), may hold values from -6 to 6
- modulation: float32 [4, 2, 5120], replicated, may hold values from -3 to 3
- controls: int32 [3], replicated, may hold values from 0 to 6, as said below
- frame_pos: int32 [11], replicated, may hold values from 0 to 63
Outputs:
- attention_out: bfloat16 [2, 352, 2560], P(None, 'seq', 'head')
- new_keys: bfloat16 [9, 352, 2560], P(None, 'seq', 'head')
- new_values: bfloat16 [9, 352, 2560], P(None, 'seq', 'head')
Inputs may be any that keep to these rules, and one draw needn't show every extreme that they name: controls[0] lies in 1 to 3, controls[1] in 0 to 6 and equal to 6 whenever controls[0] is below 3, controls[2] in 1 to 2.
All inputs are finite; a program needn't handle non-finite values.
Results may differ from a plain program's by a relative error of at most 0.011.
The roundings to bfloat16 on the way count: a program that leaves them out, or rounds other values in their place, can miss the bound.
Values may be sent and summed in bfloat16 or wider, within the bound.
A program may use at most 320 MiB of HBM per device.

v0:
```python
import jax
import jax.numpy as jnp
from jax import lax
from jax.sharding import PartitionSpec as P

HD = 128


epsilon = 1e-06


def modulate(states, modulation, step_index):
    choose = (jnp.arange(modulation.shape[0], dtype=jnp.int32) == step_index).astype(jnp.float32)
    picked = jnp.sum(choose[:, None, None] * modulation, axis=0)
    values = states.astype(jnp.float32)
    centre = jnp.mean(values, axis=-1, keepdims=True)
    spread = jnp.mean(jnp.square(values - centre), axis=-1, keepdims=True)
    normed = (values - centre) * lax.rsqrt(spread + epsilon)
    return (normed * (1.0 + picked[1]) + picked[0]).astype(jnp.bfloat16)


def rms_scale(values, square_total, width, gain):
    return values * lax.rsqrt(square_total / width + epsilon)[:, None] * gain


def rotate(values, time_pos, space_pos):
    head_size = values.shape[-1]
    half_size = head_size // 2
    time_pairs = (head_size - 4 * (head_size // 6)) // 2
    space_pairs = half_size - time_pairs
    pair_index = jnp.arange(half_size, dtype=jnp.int32)
    exponent = jnp.where(
        pair_index < time_pairs, pair_index / time_pairs, (pair_index - time_pairs) / space_pairs
    ).astype(jnp.float32)
    frequency = jnp.power(10000.0, -exponent)
    is_time = (pair_index < time_pairs)[None, None, :]
    position = jnp.where(
        is_time,
        time_pos.astype(jnp.float32)[:, None, None],
        space_pos.astype(jnp.float32)[None, :, None],
    )
    angle = position * frequency
    cosine = jnp.cos(angle)[:, :, None, :]
    sine = jnp.sin(angle)[:, :, None, :]
    first = values[..., :half_size]
    second = values[..., half_size:]
    return jnp.concatenate(
        [first * cosine - second * sine, second * cosine + first * sine], axis=-1
    )


def write_cache(key_store, value_store, fresh_keys, fresh_values, slot_start, sinks):
    rolling = key_store.shape[0] - sinks
    for group_frame in range(fresh_keys.shape[0]):
        target = sinks + (slot_start + group_frame) % rolling
        anchor = (target, jnp.int32(0), jnp.int32(0))
        key_store = lax.dynamic_update_slice(
            key_store, fresh_keys[group_frame : group_frame + 1], anchor
        )
        value_store = lax.dynamic_update_slice(
            value_store, fresh_values[group_frame : group_frame + 1], anchor
        )
    return (key_store, value_store)


def body(
    hidden_states,
    clean_states,
    w_query,
    w_key,
    w_value,
    q_gain,
    k_gain,
    cache_keys,
    cache_values,
    modulation,
    controls,
    frame_pos,
):
    timestep = controls[0]
    write_slot = controls[1]
    sink_count = controls[2]
    full_hidden, full_clean = (
        lax.all_gather(hidden_states, "head", axis=2, tiled=True),
        lax.all_gather(clean_states, "head", axis=2, tiled=True),
    )
    group_count, local_frame, model_width = full_hidden.shape
    local_rows = group_count * local_frame
    cache_count = cache_keys.shape[0]
    local_inner = w_query.shape[1]
    head_size = HD
    local_heads = local_inner // head_size
    inner_width = local_inner * lax.axis_size("head")
    noisy = modulate(full_hidden, modulation, timestep).reshape(local_rows, model_width)
    settled = modulate(full_clean, modulation, jnp.int32(0)).reshape(local_rows, model_width)
    query_raw = jnp.dot(noisy, w_query, preferred_element_type=jnp.float32)
    key_raw = jnp.dot(noisy, w_key, preferred_element_type=jnp.float32)
    key_clean = jnp.dot(settled, w_key, preferred_element_type=jnp.float32)
    value_new = jnp.dot(noisy, w_value, preferred_element_type=jnp.float32).astype(jnp.bfloat16)
    value_clean = jnp.dot(settled, w_value, preferred_element_type=jnp.float32).astype(jnp.bfloat16)
    square_query, square_key, square_clean = lax.psum(
        (
            jnp.sum(query_raw * query_raw, axis=-1),
            jnp.sum(key_raw * key_raw, axis=-1),
            jnp.sum(key_clean * key_clean, axis=-1),
        ),
        "head",
    )
    query_norm = rms_scale(query_raw, square_query, inner_width, q_gain)
    key_norm = rms_scale(key_raw, square_key, inner_width, k_gain)
    stored_keys = rms_scale(key_clean, square_clean, inner_width, k_gain).astype(jnp.bfloat16)
    space_pos = lax.axis_index("seq") * local_frame + jnp.arange(local_frame, dtype=jnp.int32)
    group_time = frame_pos[cache_count:]
    cache_time = frame_pos[:cache_count]
    query_rot = (
        rotate(
            query_norm.reshape(group_count, local_frame, local_heads, head_size),
            group_time,
            space_pos,
        )
        .astype(jnp.bfloat16)
        .reshape(group_count, local_frame, local_inner)
    )
    key_rot = (
        rotate(
            key_norm.reshape(group_count, local_frame, local_heads, head_size),
            group_time,
            space_pos,
        )
        .astype(jnp.bfloat16)
        .reshape(group_count, local_frame, local_inner)
    )
    cache_rot = (
        rotate(
            cache_keys.astype(jnp.float32).reshape(
                cache_count, local_frame, local_heads, head_size
            ),
            cache_time,
            space_pos,
        )
        .astype(jnp.bfloat16)
        .reshape(cache_count, local_frame, local_inner)
    )
    key_local = jnp.concatenate([cache_rot, key_rot], axis=0)
    value_local = jnp.concatenate(
        [cache_values, value_new.reshape(group_count, local_frame, local_inner)], axis=0
    )
    scale = head_size ** (-0.5)
    query_whole = lax.all_gather(query_rot, "seq", axis=1, tiled=True)
    all_rows = query_whole.shape[0] * query_whole.shape[1]
    scores = (
        jnp.einsum(
            "qhd,khd->hqk",
            query_whole.reshape(all_rows, local_heads, head_size),
            key_local.reshape(-1, local_heads, head_size),
            preferred_element_type=jnp.float32,
        )
        * scale
    )
    top_score = lax.pmax(jnp.max(scores, axis=-1), "seq")
    weights = jnp.exp(scores - top_score[..., None])
    totals = jnp.sum(weights, axis=-1)
    summed = jnp.einsum(
        "hqk,khd->qhd",
        weights.astype(jnp.bfloat16),
        value_local.reshape(-1, local_heads, head_size),
        preferred_element_type=jnp.float32,
    )
    summed_part, totals_part = (
        lax.psum_scatter(
            summed.reshape(group_count, -1, local_inner), "seq", scatter_dimension=1, tiled=True
        ),
        lax.psum_scatter(
            jnp.transpose(totals).reshape(group_count, -1, local_heads),
            "seq",
            scatter_dimension=1,
            tiled=True,
        ),
    )
    attended = (
        summed_part.reshape(local_rows, local_heads, head_size)
        / totals_part.reshape(local_rows, local_heads)[:, :, None]
    )
    attention_out = attended.reshape(group_count, local_frame, local_inner).astype(jnp.bfloat16)
    new_keys, new_values = write_cache(
        cache_keys,
        cache_values,
        stored_keys.reshape(group_count, local_frame, local_inner),
        value_clean.reshape(group_count, local_frame, local_inner),
        write_slot,
        sink_count,
    )
    return (attention_out, new_keys, new_values)


def solution(mesh):
    in_specs = (
        P(None, "seq", "head"),
        P(None, "seq", "head"),
        P(None, "head"),
        P(None, "head"),
        P(None, "head"),
        P("head"),
        P("head"),
        P(None, "seq", "head"),
        P(None, "seq", "head"),
        P(),
        P(),
        P(),
    )
    out_specs = (P(None, "seq", "head"), P(None, "seq", "head"), P(None, "seq", "head"))
    return jax.shard_map(body, mesh=mesh, in_specs=in_specs, out_specs=out_specs, check_vma=False)
```

profile of v0, /device:TPU:0, one launch (start us, length us, event | category | flops | bytes accessed | tf_op | source)
XLA Modules:
  0.0 270.5 jit_solution(3133796648397645756)
XLA Ops:
  7.2 1.9 copy.76
  9.2 1.1 copy.77
  11.9 1.6 fusion.26
  13.5 10.7 %all_gather.9 = bf16[2,44,5120]{2,0,1:T(2,128)(2,1)S(1)} all-gather(bf16[2,44,1280]{2,0,1:T(2,128)(2,1)S(1)} %copy-done.4), channel_id=1, replica_groups=mesh['seq'=8,'head'=4] {'head'}, dimensions={2}, use_global_device_ids=true | all-gather | bytes 1126400 | tf_op jit(solution)/shard_map/all_gather | solution.py:84
  25.0 1.3 fusion.14
  26.6 1.7 fusion.17
  28.8 4.0 %convolution_convert_fusion.1 = bf16[88,640]{1,0:T(8,128)(2,1)S(1)} fusion(bf16[88,5120]{1,0:T(8,128)(2,1)S(1)} %reshape.149, bf16[5120,640]{1,0:T(8,128)(2,1)} %param.16), kind=kOutput, calls=%fused_computation.27 | convolution fusion | flops 576773120 | bytes 7567360 | tf_op jit(solution)/shard_map/dot_general | solution.py:99
  32.8 4.2 %multiply_reduce_fusion.2 = (f32[88]{0:T(128)S(1)}, f32[88,640]{1,0:T(8,128)S(1)}) fusion(bf16[88,5120]{1,0:T(8,128)(2,1)S(1)} %reshape.149, bf16[5120,640]{1,0:T(8,128)(2,1)} %param.15), kind=kOutput, calls=%fused_computation.43 | convolution fusion | flops 576829376 | bytes 7680352 | tf_op jit(solution)/shard_map/dot_general | solution.py:97
  37.0 4.2 %multiply_reduce_fusion.3 = (f32[88]{0:T(128)S(1)}, f32[88,640]{1,0:T(8,128)S(1)}) fusion(bf16[88,5120]{1,0:T(8,128)(2,1)S(1)} %reshape.149, bf16[5120,640]{1,0:T(8,128)(2,1)} %param.14), kind=kOutput, calls=%fused_computation.45 | convolution fusion | flops 576829376 | bytes 7680352 | tf_op jit(solution)/shard_map/dot_general | solution.py:96
  41.3 1.7 reshape.151
  42.9 9.5 %all_gather.11 = bf16[2,44,5120]{2,0,1:T(2,128)(2,1)S(1)} all-gather(bf16[2,44,1280]{2,0,1:T(2,128)(2,1)S(1)} %copy-done.5), channel_id=1, replica_groups=mesh['seq'=8,'head'=4] {'head'}, dimensions={2}, use_global_device_ids=true | all-gather | bytes 1126400 | tf_op jit(solution)/shard_map/all_gather | solution.py:85
  53.2 1.3 fusion.10
  54.5 1.7 fusion.13
  56.7 4.2 %multiply_reduce_fusion.1 = (f32[88]{0:T(128)S(1)}, f32[88,640]{1,0:T(8,128)S(1)}) fusion(bf16[88,5120]{1,0:T(8,128)(2,1)S(1)} %reshape.160, bf16[5120,640]{1,0:T(8,128)(2,1)} %param.15), kind=kOutput, calls=%fused_computation.41 | convolution fusion | flops 576829376 | bytes 7680352 | tf_op jit(solution)/shard_map/dot_general | solution.py:98
  60.8 6.7 %all-reduce.2 = (f32[88]{0:T(128)S(1)}, f32[88]{0:T(128)S(1)}, f32[88]{0:T(128)S(1)}) all-reduce(f32[88]{0:T(128)S(1)} %get-tuple-element.38, f32[88]{0:T(128)S(1)} %get-tuple-element.40, f32[88]{0:T(128)S(1)} %get-tuple-element.42), channel_id=1, replica_groups=mesh['seq'=8,'head'=4] {'head'}, use_global_device_ids=true, to_apply=%region_4.0 | all-reduce | flops 264 | bytes 2112 | tf_op jit(solution)/shard_map/psum | solution.py:101
  69.0 0.8 reshape.164
  70.2 33.1 %all_gather.10 = bf16[2,352,640]{2,0,1:T(2,128)(2,1)S(1)} all-gather(bf16[2,44,640]{2,0,1:T(2,128)(2,1)S(1)} %copy.56), channel_id=1, replica_groups=mesh['seq'=8,'head'=4] {'seq'}, dimensions={1}, use_global_device_ids=true | all-gather | bytes 1013760 | tf_op jit(solution)/shard_map/all_gather | solution.py:149
  103.3 1.7 copy.43
  105.8 1.6 reshape.162
  107.4 1.7 subtract_convert_fusion
  110.3 1.7 reshape.157
  112.0 5.6 %multiply_reduce_fusion = (f32[5,704]{1,0:T(8,128)S(1)}, f32[5,704,484]{2,1,0:T(8,128)}) fusion(bf16[704,5,128]{0,2,1:T(8,128)(2,1)S(1)} %reshape.153, bf16[484,5,128]{2,1,0:T(8,128)(2,1)} %reshape.157), kind=kOutput, calls=%fused_computation.1 | convolution fusion | flops 439545920 | bytes 8349440 | tf_op jit(solution)/shard_map/qhd,khd->hqk/dot_general | solution.py:152
  117.7 36.5 %pmax.7 = f32[5,704]{1,0:T(8,128)S(1)} all-reduce(f32[5,704]{1,0:T(8,128)S(1)} %get-tuple-element.44), channel_id=1, replica_groups=mesh['seq'=8,'head'=4] {'seq'}, use_global_device_ids=true, to_apply=%region_8.0 | all-reduce | flops 3520 | bytes 28160 | tf_op jit(solution)/shard_map/pmax | solution.py:160
  154.2 5.7 %fusion.18 = f32[704,5,128]{2,0,1:T(8,128)} fusion(f32[5,704,484]{2,1,0:T(8,128)} %get-tuple-element.45, f32[5,704]{1,0:T(8,128)S(1)} %pmax.7, bf16[484,5,128]{2,1,0:T(8,128)(2,1)S(1)} %copy-done), kind=kOutput, calls=%fused_computation.25 | convolution fusion | flops 441253120 | bytes 9250560 | tf_op jit(solution)/shard_map/hqk,khd->qhd/dot_general | solution.py:163
  159.9 1.9 copy.49
  161.8 2.9 %reshape.158 = f32[2,352,640]{1,0,2:T(2,128)} reshape(f32[704,5,128]{0,2,1:T(8,128)S(1)} %copy.49) | data formatting | bytes 3604480 | tf_op jit(solution)/shard_map/reshape | solution.py:171
  164.7 4.7 %copy.50 = f32[2,352,640]{2,0,1:T(2,128)} copy(f32[2,352,640]{1,0,2:T(2,128)} %reshape.158) | data formatting | bytes 3604480 | tf_op jit(solution)/shard_map/reshape | solution.py:171
  172.4 4.8 %fusion = f32[5,704]{1,0:T(8,128)S(1)} fusion(f32[5,704,484]{2,1,0:T(8,128)} %get-tuple-element.45, f32[5,704]{1,0:T(8,128)S(1)} %pmax.7), kind=kLoop, calls=%fused_computation.2 | loop fusion | flops 5107520 | bytes 6842880 | tf_op jit(solution)/shard_map/reduce_sum | solution.py:162
  178.5 33.9 %all-reduce.1 = f32[2,352,5]{1,0,2:T(2,128)S(1)} all-reduce(f32[2,352,5]{1,0,2:T(2,128)S(1)} %reshape.159), channel_id=3, replica_groups=mesh['seq'=8,'head'=4] {'seq'}, use_global_device_ids=true, to_apply=%region_11.0.clone | all-reduce | flops 3520 | bytes 28160
  212.8 4.1 %convolution_convert_fusion = bf16[88,640]{1,0:T(8,128)(2,1)S(1)} fusion(bf16[88,5120]{1,0:T(8,128)(2,1)S(1)} %reshape.160, bf16[5120,640]{1,0:T(8,128)(2,1)} %param.16), kind=kOutput, calls=%fused_computation.26 | convolution fusion | flops 576773120 | bytes 7567360 | tf_op jit(solution)/shard_map/dot_general | solution.py:100
  219.5 42.4 %all-reduce.5.cloned.1.call-done = f32[2,352,640]{2,0,1:T(2,128)} async-done(((f32[2,352,640]{2,0,1:T(2,128)}), f32[2,352,640]{2,0,1:T(2,128)}) %all-reduce.5.cloned.1.call-update) | async-done | bytes 1802256
  261.9 1.0 constant_dynamic-slice_fusion.1
  (78 shorter events, 12.7 us)
Async XLA Ops:
  7.2 6.4 %copy-start.4 = (bf16[2,44,1280]{2,0,1:T(2,128)(2,1)S(1)}, bf16[2,44,1280]{2,0,1:T(2,128)(2,1)}, u32[]{:S(2)}) copy-start(bf16[2,44,1280]{2,0,1:T(2,128)(2,1)} %param.12) | copy-start | bytes 675844
  7.2 3.2 %copy-start.7 = (s32[3]{0:T(128)S(1)}, s32[3]{0:T(128)}, u32[]{:S(2)}) copy-start(s32[3]{0:T(128)} %param.22) | copy-start | bytes 40
  7.2 3.1 %copy-start.10 = (s32[11]{0:T(128)S(1)}, s32[11]{0:T(128)}, u32[]{:S(2)}) copy-start(s32[11]{0:T(128)} %param.23) | copy-start | bytes 136
  7.2 254.7 %all-reduce.5.cloned.1.call-start = ((), (), s32[]{:S(2)}) async-start(), calls=%async_computation | async-start | bytes 3604480
  10.2 30.9 %copy-start.1 = (bf16[9,44,640]{2,1,0:T(8,128)(2,1)}, bf16[9,44,640]{2,1,0:T(8,128)(2,1)S(1)}, u32[]{:S(2)}) copy-start(bf16[9,44,640]{2,1,0:T(8,128)(2,1)S(1)} %copy.77) | copy-start | bytes 1520644
  11.6 14.7 %copy-start.6 = (f32[4,2,5120]{2,1,0:T(2,128)S(1)}, f32[4,2,5120]{2,1,0:T(2,128)}, u32[]{:S(2)}) copy-start(f32[4,2,5120]{2,1,0:T(2,128)} %param.21) | copy-start | bytes 491524
  41.2 1.8 copy-start.5
  56.6 10.9 %copy-start.8 = (f32[640]{0:T(1024)S(1)}, f32[640]{0:T(1024)}, u32[]{:S(2)}) copy-start(f32[640]{0:T(1024)} %param.18) | copy-start | bytes 7684
  56.7 11.7 %copy-start.9 = (f32[640]{0:T(1024)S(1)}, f32[640]{0:T(1024)}, u32[]{:S(2)}) copy-start(f32[640]{0:T(1024)} %param.17) | copy-start | bytes 7684
  109.1 1.2 copy-start.3
  112.0 42.1 %copy-start = (bf16[484,5,128]{2,1,0:T(8,128)(2,1)S(1)}, bf16[484,5,128]{2,1,0:T(8,128)(2,1)}, u32[]{:S(2)}) copy-start(bf16[484,5,128]{2,1,0:T(8,128)(2,1)} %reshape.151) | copy-start | bytes 1858564
  172.4 4.9 %copy-start.11 = (u32[32]{0:T(128)S(1)}, u32[32]{0:T(128)}, u32[]{:S(2)}) copy-start(u32[32]{0:T(128)} %constant.61) | copy-start | bytes 388
  212.8 4.7 %copy-start.2 = (bf16[88,640]{1,0:T(8,128)(2,1)S(1)}, bf16[88,640]{1,0:T(8,128)(2,1)}, u32[]{:S(2)}) copy-start(bf16[88,640]{1,0:T(8,128)(2,1)} %get-tuple-element.29) | copy-start | bytes 337924
Sparse Core Ops, SparseCore 0:
  169.5 92.3 all-reduce.4
where the time goes:
time: 271 us; the launch traced here: 270 us
  blocking collectives  130 us (48%)
  waiting for transfers between devices  42.4 us (16%)
  matrix products  32 us (12%)
  local copies, waits for them, and re-layouts  28.4 us (10%)
  other arithmetic  19.3 us (7%)
  between operations  18.1 us (7%)
    unnamed x2, waiting for transfers between devices  42.4 us
    pmax x1, blocking collectives, body(): top_score = lax.pmax(jnp.max(scores, axis=-1), 'seq')  36.5 us
    unnamed x1, blocking collectives  33.9 us
    all_gather x1, blocking collectives, body(): query_whole = lax.all_gather(query_rot, 'seq', axis=1, tiled=True)  33.1 us
    all_gather x1, blocking collectives, body(): lax.all_gather(hidden_states, 'head', axis=2, tiled=True)  10.7 us
    all_gather x1, blocking collectives, body(): lax.all_gather(clean_states, 'head', axis=2, tiled=True)  9.48 us
    reshape x2, local copies, waits for them, and re-layouts, body(): summed.reshape(group_count, -1, local_inner)  7.56 us
    psum x1, blocking collectives, body(): lax.psum((jnp.sum(query_raw * query_raw, axis=-1), jnp.sum(key_raw * key_...  6.68 us
  transfers between devices with their start and end apart: 1, of which 1 were waited for; matrix products, arithmetic and copies ran while one was open for 5% of the time, Pallas kernels for 0%

commit v1 on v0

v1 whole, which is shorter than its diff:
```python
import functools

import jax
import jax.numpy as jnp
import numpy as np
from jax import lax
from jax.experimental import pallas as pl
from jax.experimental.pallas import tpu as pltpu
from jax.sharding import PartitionSpec as P

HD = 128
epsilon = 1e-06
NX = 2
F32 = jnp.float32
BF16 = jnp.bfloat16


def kernel(
    n_seq,
    n_head,
    x_noisy,
    x_clean,
    w_query,
    w_key,
    w_value,
    q_gain,
    k_gain,
    cache_keys,
    cache_values,
    modulation,
    frequency,
    controls,
    frame_pos,
    out_ref,
    new_keys,
    new_values,
    w_vmem,
    xg,
    y,
    acc,
    acc_b,
    table,
    k32,
    v32,
    kb,
    vb,
    q_buf,
    part_send,
    part_recv,
    stat_send,
    stat_recv,
    ss_send,
    ss_recv,
    w_sem,
    x_send_sem,
    x_fwd_sem,
    x_recv_sem,
    ss_send_sem,
    ss_recv_sem,
    q_send_sem,
    q_fwd_sem,
    q_recv_sem,
    p_send_sem,
    p_recv_sem,
    t_send_sem,
    t_recv_sem,
):
    seq = lax.axis_index("seq")
    head = lax.axis_index("head")
    groups, frame, shard = x_noisy.shape
    padded = y.shape[2] // groups
    rows = groups * padded
    caches = cache_keys.shape[0]
    inner = w_query.shape[1]
    heads = inner // HD
    n_keys = (caches + groups) * frame
    key_rows = k32.shape[0]
    width = inner * n_head
    model = shard * n_head
    n_z = n_seq // NX
    n_y = n_head // 2
    z = seq // NX
    x = seq % NX
    mate_x = z * NX + (1 - x)
    core = head % 2
    yy = head // 2
    mate = yy * 2 + (1 - core)

    barrier = pltpu.get_barrier_semaphore()
    for step in range(1, n_head):
        pl.semaphore_signal(
            barrier, inc=1, device_id={"head": lax.rem(head + step, n_head)},
            device_id_type=pl.DeviceIdType.MESH,
        )
    for step in range(1, n_seq):
        pl.semaphore_signal(
            barrier, inc=1, device_id={"seq": lax.rem(seq + step, n_seq)},
            device_id_type=pl.DeviceIdType.MESH,
        )
    w_copies = [
        pltpu.make_async_copy(w, w_vmem.at[i], w_sem.at[i])
        for i, w in enumerate((w_query, w_key, w_value))
    ]
    for copy in w_copies:
        copy.start()
    pl.semaphore_wait(barrier, n_head - 1 + n_seq - 1)

    def remote(src, dst, send, recv, axis, index):
        return pltpu.make_async_remote_copy(
            src_ref=src, dst_ref=dst, send_sem=send, recv_sem=recv,
            device_id={axis: index}, device_id_type=pl.DeviceIdType.MESH,
        )

    def x_copy(kind, source, slot, send, to):
        return remote(source, xg.at[kind, slot], send, x_recv_sem.at[kind, slot], "head", to)

    own_x = (x_noisy, x_clean)
    x_sends = []
    for kind in range(2):
        for step in range(1, n_y):
            to = lax.rem(yy + step, n_y) * 2 + core
            x_sends.append(x_copy(kind, own_x[kind], head, x_send_sem.at[kind, step], to))
            x_sends[-1].start()
        x_sends.append(x_copy(kind, own_x[kind], head, x_send_sem.at[kind, 0], mate))
        x_sends[-1].start()
        xg[kind, head] = own_x[kind][...]

    y[...] = jnp.zeros_like(y)
    k32[n_keys:, :] = jnp.zeros((key_rows - n_keys, inner), F32)
    v32[n_keys:, :] = jnp.zeros((key_rows - n_keys, inner), F32)

    lane = lax.broadcasted_iota(jnp.int32, (padded, HD), 1)
    half = HD // 2
    time_pairs = (HD - 4 * (HD // 6)) // 2
    is_time = (lane % half) < time_pairs
    sign = jnp.where(lane < half, -1.0, 1.0).astype(F32)
    freq = frequency[0:1, :]
    space = (lax.broadcasted_iota(jnp.int32, (padded, HD), 0) + seq * frame).astype(F32)
    space_angle = space * freq
    space_cos = jnp.cos(space_angle)
    space_sin = jnp.sin(space_angle) * sign
    time_row = lax.broadcasted_iota(jnp.int32, (16, HD), 0)
    times = jnp.zeros((16, HD), F32)
    for f in range(caches + groups):
        times = jnp.where(time_row == f, frame_pos[f].astype(F32), times)
    time_angle = times * freq
    time_cos = jnp.cos(time_angle)
    time_sin = jnp.sin(time_angle) * sign[0:1, :]
    for f in range(caches + groups):
        table[f, 0] = jnp.where(is_time, time_cos[f : f + 1, :], space_cos)
        table[f, 1] = jnp.where(is_time, time_sin[f : f + 1, :], space_sin)

    def rotate(values, f, count):
        return values * table[f, 0, :count, :] + pltpu.roll(values, half, 1) * table[f, 1, :count, :]

    for f in range(caches):
        for h in range(heads):
            cols = slice(h * HD, (h + 1) * HD)
            at = slice(f * frame, (f + 1) * frame)
            k32[at, cols] = rotate(cache_keys[f, :, cols].astype(F32), f, frame)
            v32[at, cols] = cache_values[f, :, cols].astype(F32)

    def gather_x(kind):
        forwards = []
        for step in range(1, n_y):
            source = lax.rem(yy + n_y - step, n_y) * 2 + core
            x_copy(kind, own_x[kind], source, x_send_sem.at[kind, 0], mate).wait_recv()
            forwards.append(
                x_copy(kind, xg.at[kind, source], source, x_fwd_sem.at[kind, step], mate)
            )
            forwards[-1].start()
        for step in range(n_y):
            source = lax.rem(yy + n_y - step, n_y) * 2 + (1 - core)
            x_copy(kind, own_x[kind], source, x_send_sem.at[kind, 0], mate).wait_recv()
        return forwards

    def modulate(kind, step_index):
        def pick(part, columns):
            chosen = jnp.zeros((1, shard), F32)
            for i in range(modulation.shape[0]):
                chosen = jnp.where(step_index == i, modulation[i, part : part + 1, columns], chosen)
            return chosen

        for g in range(groups):
            total = jnp.zeros((frame, 1), F32)
            for j in range(n_head):
                total += jnp.sum(xg[kind, j, g].astype(F32), axis=-1, keepdims=True)
            centre = total / model
            total = jnp.zeros((frame, 1), F32)
            for j in range(n_head):
                away = xg[kind, j, g].astype(F32) - centre
                total += jnp.sum(away * away, axis=-1, keepdims=True)
            inverse = lax.rsqrt(total / model + epsilon)
            for j in range(n_head):
                columns = slice(j * shard, (j + 1) * shard)
                normed = (xg[kind, j, g].astype(F32) - centre) * inverse
                result = normed * (1.0 + pick(1, columns)) + pick(0, columns)
                y[kind, j, g * padded : g * padded + frame, :] = result.astype(BF16)

    def project(kind, which, target):
        target[...] = jnp.zeros_like(target)

        @pl.loop(0, n_head)
        def _(j):
            begin = pl.multiple_of(j * shard, shard)
            target[...] += jnp.dot(
                y[kind, j], w_vmem[which, pl.ds(begin, shard), :], preferred_element_type=F32
            )

    lanes = lax.broadcasted_iota(jnp.int32, (rows, HD), 1)

    def share_squares(kind, squares):
        ss_send[kind] = squares
        copies = []
        for step in range(1, n_head):
            to = lax.rem(head + step, n_head)
            copies.append(
                remote(
                    ss_send.at[kind], ss_recv.at[kind, head], ss_send_sem.at[kind, step],
                    ss_recv_sem.at[kind, head], "head", to,
                )
            )
            copies[-1].start()
        return copies

    def total_squares(kind, squares):
        for step in range(1, n_head):
            source = lax.rem(head + step, n_head)
            remote(
                ss_send.at[kind], ss_recv.at[kind, source], ss_send_sem.at[kind, step],
                ss_recv_sem.at[kind, source], "head", source,
            ).wait_recv()
            squares = squares + ss_recv[kind, source]
        return lax.rsqrt(squares / width + epsilon)

    forwards = gather_x(0)
    modulate(0, controls[0])
    w_copies[0].wait()
    project(0, 0, acc)
    w_copies[1].wait()
    project(0, 1, acc_b)
    query_squares = jnp.sum(acc[...] * acc[...], axis=-1, keepdims=True)
    key_squares = jnp.sum(acc_b[...] * acc_b[...], axis=-1, keepdims=True)
    squares = jnp.where(lanes == 0, query_squares, key_squares)
    ss_copies = share_squares(0, squares)
    inverse = total_squares(0, squares)
    for g in range(groups):
        at = slice(g * padded, (g + 1) * padded)
        query_scale = inverse[at, 0:1]
        for h in range(heads):
            cols = slice(h * HD, (h + 1) * HD)
            normed = acc[at, cols] * query_scale * q_gain[:, cols]
            q_buf[seq, at, cols] = rotate(normed, caches + g, padded).astype(BF16)

    def q_copy(source, send, to):
        return remote(q_buf.at[source], q_buf.at[source], send, q_recv_sem.at[source], "seq", to)

    q_sends = []
    for step in range(1, n_z):
        q_sends.append(q_copy(seq, q_send_sem.at[step], lax.rem(z + step, n_z) * NX + x))
        q_sends[-1].start()
    q_sends.append(q_copy(seq, q_fwd_sem.at[0], mate_x))
    q_sends[-1].start()

    for g in range(groups):
        at = slice(g * padded, (g + 1) * padded)
        key_scale = inverse[at, 1:2]
        place = slice((caches + g) * frame, (caches + g + 1) * frame)
        for h in range(heads):
            cols = slice(h * HD, (h + 1) * HD)
            normed = acc_b[at, cols] * key_scale * k_gain[:, cols]
            k32[place, cols] = rotate(normed, caches + g, padded)[:frame, :]
    w_copies[2].wait()
    project(0, 2, acc)
    for g in range(groups):
        place = slice((caches + g) * frame, (caches + g + 1) * frame)
        v32[place, :] = acc[g * padded : g * padded + frame, :]
    kb[...] = k32[...].astype(BF16)
    vb[...] = v32[...].astype(BF16)

    forwards += gather_x(1)
    modulate(1, jnp.int32(0))
    project(1, 1, acc_b)
    squares = jnp.broadcast_to(jnp.sum(acc_b[...] * acc_b[...], axis=-1, keepdims=True), (rows, HD))
    ss_copies += share_squares(1, squares)
    project(1, 2, acc)

    scale = HD ** (-0.5)
    column = lax.broadcasted_iota(jnp.int32, (rows, key_rows), 1)

    def attend(source, part, stat):
        stats = jnp.zeros((rows, HD), F32)
        for h in range(heads):
            cols = slice(h * HD, (h + 1) * HD)
            scores = lax.dot_general(
                q_buf[source, :, cols], kb[:, cols], (((1,), (1,)), ((), ())),
                preferred_element_type=F32,
            ) * scale
            scores = jnp.where(column < n_keys, scores, -3.0e38)
            top = jnp.max(scores, axis=-1, keepdims=True)
            weights = jnp.exp(scores - top)
            total = jnp.sum(weights, axis=-1, keepdims=True)
            part[:, cols] = jnp.dot(
                weights.astype(BF16), vb[:, cols], preferred_element_type=F32
            ).astype(BF16)
            stats = jnp.where(lanes == h, top, stats)
            stats = jnp.where(lanes == half + h, total, stats)
        stat[...] = stats

    def part_copy(slot, to):
        return (
            remote(
                part_send.at[to], part_recv.at[slot], p_send_sem.at[to], p_recv_sem.at[slot],
                "seq", to,
            ),
            remote(
                stat_send.at[to], stat_recv.at[slot], t_send_sem.at[to], t_recv_sem.at[slot],
                "seq", to,
            ),
        )

    @pl.loop(0, n_seq)
    def _(c):
        step = c // NX
        across = c % NX
        there = lax.rem(z + n_z - step, n_z) * NX
        source = there + lax.rem(x + across, NX)

        @pl.when(c > 0)
        def _():
            q_copy(source, q_send_sem.at[0], mate_x).wait_recv()

        @pl.when((c > 0) & (across == 0))
        def _():
            q_copy(source, q_fwd_sem.at[step], mate_x).start()

        attend(source, part_send.at[source], stat_send.at[source])

        @pl.when(c > 0)
        def _():
            for copy in part_copy(seq, source):
                copy.start()

    part_recv[seq] = part_send[seq]
    stat_recv[seq] = stat_send[seq]

    inverse = total_squares(1, squares)
    rolling = caches - controls[2]
    targets = [controls[2] + lax.rem(controls[1] + g, rolling) for g in range(groups)]
    for h in range(heads):
        cols = slice(h * HD, (h + 1) * HD)
        fresh = []
        for g in range(groups):
            at = slice(g * padded, (g + 1) * padded)
            normed = acc_b[at, cols] * inverse[at, 0:1] * k_gain[:, cols]
            fresh.append(
                (normed[:frame, :].astype(BF16), acc[at, cols][:frame, :].astype(BF16))
            )
        for f in range(caches):
            keys = cache_keys[f, :, cols]
            values = cache_values[f, :, cols]
            for g in range(groups):
                keys = jnp.where(targets[g] == f, fresh[g][0], keys)
                values = jnp.where(targets[g] == f, fresh[g][1], values)
            new_keys[f, :, cols] = keys
            new_values[f, :, cols] = values

    @pl.loop(1, n_seq)
    def _(c):
        source = lax.rem(seq + c, n_seq)
        for copy in part_copy(source, source):
            copy.wait_recv()

    def highest(j, top):
        return jnp.maximum(top, stat_recv[j])

    top = lax.fori_loop(1, n_seq, highest, stat_recv[0])

    def summed(j, total):
        stat = stat_recv[j]
        weight = jnp.exp(stat - top)
        for h in range(heads):
            cols = slice(h * HD, (h + 1) * HD)
            acc[:, cols] += part_recv[j, :, cols].astype(F32) * weight[:, h : h + 1]
        return total + weight * pltpu.roll(stat, half, 1)

    acc[...] = jnp.zeros_like(acc)
    total = lax.fori_loop(0, n_seq, summed, jnp.zeros((rows, HD), F32))
    for h in range(heads):
        cols = slice(h * HD, (h + 1) * HD)
        result = (acc[:, cols] / total[:, h : h + 1]).astype(BF16)
        for g in range(groups):
            out_ref[g, :, cols] = result[g * padded : g * padded + frame, :]

    for copy in x_sends + forwards + ss_copies + q_sends:
        copy.wait_send()

    @pl.loop(1, n_z)
    def _(step):
        source = lax.rem(z + n_z - step, n_z) * NX + x
        q_copy(source, q_fwd_sem.at[step], mate_x).wait_send()

    @pl.loop(1, n_seq)
    def _(c):
        source = lax.rem(seq + c, n_seq)
        for copy in part_copy(seq, source):
            copy.wait_send()


def body(n_seq, n_head, hidden, clean, w_query, w_key, w_value, q_gain, k_gain, keys, values,
         modulation, controls, frame_pos):
    groups, frame, shard = hidden.shape
    caches = keys.shape[0]
    inner = w_query.shape[1]
    padded = -(-frame // 16) * 16
    rows = groups * padded
    key_rows = -(-((caches + groups) * frame) // 128) * 128
    half = HD // 2
    time_pairs = (HD - 4 * (HD // 6)) // 2
    pair = np.arange(half)
    exponent = np.where(pair < time_pairs, pair / time_pairs, (pair - time_pairs) / (half - time_pairs))
    line = np.power(10000.0, -exponent).astype(np.float32)
    frequency = jnp.asarray(np.tile(np.concatenate([line, line])[None, :], (8, 1)))
    vmem = pl.BlockSpec(memory_space=pltpu.VMEM)
    smem = pl.BlockSpec(memory_space=pltpu.SMEM)
    hbm = pl.BlockSpec(memory_space=pl.ANY)
    dma = pltpu.SemaphoreType.DMA
    return pl.pallas_call(
        functools.partial(kernel, n_seq, n_head),
        out_shape=(
            jax.ShapeDtypeStruct((groups, frame, inner), BF16),
            jax.ShapeDtypeStruct(keys.shape, BF16),
            jax.ShapeDtypeStruct(values.shape, BF16),
        ),
        in_specs=[vmem, vmem, hbm, hbm, hbm, vmem, vmem, vmem, vmem, vmem, vmem, smem, smem],
        out_specs=(vmem, vmem, vmem),
        scratch_shapes=[
            pltpu.VMEM((3,) + w_query.shape, BF16),
            pltpu.VMEM((2, n_head, groups, frame, shard), BF16),
            pltpu.VMEM((2, n_head, rows, shard), BF16),
            pltpu.VMEM((rows, inner), F32),
            pltpu.VMEM((rows, inner), F32),
            pltpu.VMEM((caches + groups, 2, padded, HD), F32),
            pltpu.VMEM((key_rows, inner), F32),
            pltpu.VMEM((key_rows, inner), F32),
            pltpu.VMEM((key_rows, inner), BF16),
            pltpu.VMEM((key_rows, inner), BF16),
            pltpu.VMEM((n_seq, rows, inner), BF16),
            pltpu.VMEM((n_seq, rows, inner), BF16),
            pltpu.VMEM((n_seq, rows, inner), BF16),
            pltpu.VMEM((n_seq, rows, HD), F32),
            pltpu.VMEM((n_seq, rows, HD), F32),
            pltpu.VMEM((2, rows, HD), F32),
            pltpu.VMEM((2, n_head, rows, HD), F32),
            dma((3,)),
            dma((2, n_head)),
            dma((2, n_head)),
            dma((2, n_head)),
            dma((2, n_head)),
            dma((2, n_head)),
            dma((n_seq,)),
            dma((n_seq,)),
            dma((n_seq,)),
            dma((n_seq,)),
            dma((n_seq,)),
            dma((n_seq,)),
            dma((n_seq,)),
        ],
        compiler_params=pltpu.CompilerParams(
            collective_id=0, has_side_effects=True, vmem_limit_bytes=60 * 1024 * 1024
        ),
        name="block",
    )(hidden, clean, w_query, w_key, w_value, q_gain[None, :], k_gain[None, :], keys, values,
      modulation, frequency, controls, frame_pos)


def solution(mesh):
    split = P(None, "seq", "head")
    columns = P(None, "head")
    in_specs = (
        split, split, columns, columns, columns, P("head"), P("head"), split, split, P(), P(), P(),
    )
    step = functools.partial(body, mesh.shape["seq"], mesh.shape["head"])
    return jax.shard_map(
        step, mesh=mesh, in_specs=in_specs, out_specs=(split, split, split), check_vma=False
    )
```

time: 271 us -> 87.7 us (0.32)
  blocking collectives: 130 us -> 0 us
  Pallas kernels: 0 us -> 75.4 us
  waiting for transfers between devices: 42.4 us -> 0 us
  matrix products: 32 us -> 0 us
  other arithmetic: 19.3 us -> 0 us
  between operations: 18.1 us -> 0.64 us
  local copies, waits for them, and re-layouts: 28.4 us -> 11.3 us
    pallas_call x0 -> x1, Pallas kernels: none -> 75.4 us  [body(): pl.pallas_call(functools.partial(kernel, n_seq, n_head), out_shape=(jax.S...]
    all_gather x3 -> x0, blocking collectives: 53.3 us -> none  [the longest x1 33.1 us: body(): query_whole = lax.all_gather(query_rot, 'seq', axis=1, tiled=True)]
    unnamed x2 -> x0, waiting for transfers between devices: 42.4 us -> none
    pmax x1 -> x0, blocking collectives: 36.5 us -> none  [body(): top_score = lax.pmax(jnp.max(scores, axis=-1), 'seq')]
    unnamed x1 -> x0, blocking collectives: 33.9 us -> none
    dot_general x7 -> x0, matrix products: 32 us -> none  [the longest x1 5.74 us: body(): jnp.einsum('hqk,khd->qhd', weights.astype(jnp.bfloat16), value_local.resh...]
    reshape x12 -> x0, local copies, waits for them, and re-layouts: 13.9 us -> none  [the longest x2 7.56 us: body(): summed.reshape(group_count, -1, local_inner)]
    reduce_sum x6 -> x0, other arithmetic: 9.18 us -> none  [the longest x1 4.78 us: body(): totals = jnp.sum(weights, axis=-1)]
  transfers between devices with their start and end apart: 1 -> 0, of which waited for: 1 -> 0; matrix products, arithmetic and copies ran while one was open for 5% -> 0% of each run, Pallas kernels for 0% -> 0%
where the time goes in v1:
time: 87.7 us; the launch traced here: 87.3 us
  Pallas kernels  75.4 us (86%)
  local copies, waits for them, and re-layouts  11.3 us (13%)
    pallas_call x1, Pallas kernels, body(): pl.pallas_call(functools.partial(kernel, n_seq, n_head), out_shape=(jax.S...  75.4 us
    unnamed x4, local copies, waits for them, and re-layouts  7.11 us

profile of v1, /device:TPU:0, one launch (start us, length us, event | category | flops | bytes accessed | tf_op | source)
XLA Modules:
  0.0 87.3 jit_solution(13850682118962864080)
XLA Ops:
  0.6 1.3 %broadcast_in_dim.6.q_gain = f32[1,640]{1,0:T(1,128)} reshape(f32[640]{0:T(1024)} %param.18) | data formatting | bytes 5120 | tf_op jit(solution)/shard_map/broadcast_in_dim | solution.py:473
  1.9 1.3 %broadcast_in_dim.7.k_gain = f32[1,640]{1,0:T(1,128)} reshape(f32[640]{0:T(1024)} %param.19) | data formatting | bytes 5120 | tf_op jit(solution)/shard_map/broadcast_in_dim | solution.py:473
  3.2 1.7 %copy.16.x_noisy = bf16[2,44,1280]{2,1,0:T(8,128)(2,1)} copy(bf16[2,44,1280]{2,0,1:T(2,128)(2,1)} %param.13) | data formatting | bytes 450560 | tf_op args[0]
  4.8 1.7 %copy.17.x_clean = bf16[2,44,1280]{2,1,0:T(8,128)(2,1)} copy(bf16[2,44,1280]{2,0,1:T(2,128)(2,1)} %param.14) | data formatting | bytes 450560 | tf_op args[1]
  6.5 75.4 %block.1 = (bf16[2,44,640]{2,1,0:T(8,128)(2,1)}, bf16[9,44,640]{2,1,0:T(8,128)(2,1)}, bf16[9,44,640]{2,1,0:T(8,128)(2,1)}) custom-call(bf16[2,44,1280]{2,1,0:T(8,128)(2,1)} %copy.16.x_noisy, bf16[2,44,1280]{2,1,0:T(8,128)(2,1)} %copy.17.x_clean, bf16[5120,640]{1,0:T(8,128)(2,1)} %w_query.1, bf16[5120,640]{1,0:T(8,128)(2,1)} %w_key.1, ...), custom_call_target="tpu_custom_call" | custom-call | tf_op jit(solution)/shard_map/block/pallas_call | solution.py:428
  81.9 1.6 %copy.18 = bf16[2,44,640]{2,0,1:T(2,128)(2,1)} copy(bf16[2,44,640]{2,1,0:T(8,128)(2,1)} %get-tuple-element.3) | data formatting | bytes 225280 | tf_op jit(solution)/shard_map/block/pallas_call | solution.py:428
  83.5 1.9 %copy.21 = bf16[9,44,640]{2,1,0:T(8,128)(2,1)} copy(bf16[9,44,640]{2,1,0:T(8,128)(2,1)} %get-tuple-element.10) | data formatting | bytes 1013760
  85.4 1.9 %copy.22 = bf16[9,44,640]{2,1,0:T(8,128)(2,1)} copy(bf16[9,44,640]{2,1,0:T(8,128)(2,1)} %get-tuple-element.11) | data formatting | bytes 1013760

commit v2 on v1

--- a/solution.py
+++ b/solution.py
@@ -32,9 +32,12 @@
     controls,
     frame_pos,
     out_ref,
-    new_keys,
-    new_values,
+    fresh_keys,
+    fresh_values,
     w_vmem,
+    mod_vmem,
+    keys_vmem,
+    values_vmem,
     xg,
     y,
     acc,
@@ -51,7 +54,14 @@
     stat_recv,
     ss_send,
     ss_recv,
+    own_part,
+    own_stat,
+    part_mate,
+    stat_mate,
+    mate_in,
+    mate_stat,
     w_sem,
+    in_sem,
     x_send_sem,
     x_fwd_sem,
     x_recv_sem,
@@ -64,6 +74,10 @@
     p_recv_sem,
     t_send_sem,
     t_recv_sem,
+    m_send_sem,
+    m_recv_sem,
+    mt_send_sem,
+    mt_recv_sem,
 ):
     seq = lax.axis_index("seq")
     head = lax.axis_index("head")
@@ -77,6 +91,7 @@
     key_rows = k32.shape[0]
     width = inner * n_head
     model = shard * n_head
+    link_rows = ss_send.shape[-1]
     n_z = n_seq // NX
     n_y = n_head // 2
     z = seq // NX
@@ -101,6 +116,15 @@
         pltpu.make_async_copy(w, w_vmem.at[i], w_sem.at[i])
         for i, w in enumerate((w_query, w_key, w_value))
     ]
+    in_copies = [
+        pltpu.make_async_copy(source, target, in_sem.at[i])
+        for i, (source, target) in enumerate((
+            (x_noisy, xg.at[0, head]), (x_clean, xg.at[1, head]), (modulation, mod_vmem),
+            (cache_keys, keys_vmem), (cache_values, values_vmem),
+        ))
+    ]
+    for copy in in_copies:
+        copy.start()
     for copy in w_copies:
         copy.start()
     pl.semaphore_wait(barrier, n_head - 1 + n_seq - 1)
@@ -123,7 +147,6 @@
             x_sends[-1].start()
         x_sends.append(x_copy(kind, own_x[kind], head, x_send_sem.at[kind, 0], mate))
         x_sends[-1].start()
-        xg[kind, head] = own_x[kind][...]
 
     y[...] = jnp.zeros_like(y)
     k32[n_keys:, :] = jnp.zeros((key_rows - n_keys, inner), F32)
@@ -153,12 +176,14 @@
     def rotate(values, f, count):
         return values * table[f, 0, :count, :] + pltpu.roll(values, half, 1) * table[f, 1, :count, :]
 
+    in_copies[3].wait()
+    in_copies[4].wait()
     for f in range(caches):
         for h in range(heads):
             cols = slice(h * HD, (h + 1) * HD)
             at = slice(f * frame, (f + 1) * frame)
-            k32[at, cols] = rotate(cache_keys[f, :, cols].astype(F32), f, frame)
-            v32[at, cols] = cache_values[f, :, cols].astype(F32)
+            k32[at, cols] = rotate(keys_vmem[f, :, cols].astype(F32), f, frame)
+            v32[at, cols] = values_vmem[f, :, cols].astype(F32)
 
     def gather_x(kind):
         forwards = []
@@ -177,8 +202,8 @@
     def modulate(kind, step_index):
         def pick(part, columns):
             chosen = jnp.zeros((1, shard), F32)
-            for i in range(modulation.shape[0]):
-                chosen = jnp.where(step_index == i, modulation[i, part : part + 1, columns], chosen)
+            for i in range(mod_vmem.shape[0]):
+                chosen = jnp.where(step_index == i, mod_vmem[i, part : part + 1, columns], chosen)
             return chosen
 
         for g in range(groups):
@@ -209,8 +234,18 @@
 
     lanes = lax.broadcasted_iota(jnp.int32, (rows, HD), 1)
 
-    def share_squares(kind, squares):
-        ss_send[kind] = squares
+    def to_link(stats):
+        tall = jnp.concatenate([stats, jnp.zeros((link_rows - rows, HD), F32)], axis=0)
+        return tall.T[:16, :]
+
+    def from_link(flat):
+        tall = jnp.concatenate([flat, jnp.zeros((HD - 16, link_rows), F32)], axis=0)
+        return tall.T[:rows, :]
+
+    def share_squares(kind, values):
+        squares = jnp.sum(values * values, axis=-1, keepdims=True)
+        flat = to_link(jnp.broadcast_to(squares, (rows, HD)))
+        ss_send[kind] = flat
         copies = []
         for step in range(1, n_head):
             to = lax.rem(head + step, n_head)
@@ -221,7 +256,7 @@
                 )
             )
             copies[-1].start()
-        return copies
+        return copies, flat
 
     def total_squares(kind, squares):
         for step in range(1, n_head):
@@ -231,25 +266,25 @@
                 ss_recv_sem.at[kind, source], "head", source,
             ).wait_recv()
             squares = squares + ss_recv[kind, source]
-        return lax.rsqrt(squares / width + epsilon)
-
+        return from_link(lax.rsqrt(squares / width + epsilon))[:, 0:1]
+
+    in_copies[0].wait()
+    in_copies[2].wait()
     forwards = gather_x(0)
     modulate(0, controls[0])
     w_copies[0].wait()
     project(0, 0, acc)
+    ss_copies, squares = share_squares(0, acc[...])
     w_copies[1].wait()
     project(0, 1, acc_b)
-    query_squares = jnp.sum(acc[...] * acc[...], axis=-1, keepdims=True)
-    key_squares = jnp.sum(acc_b[...] * acc_b[...], axis=-1, keepdims=True)
-    squares = jnp.where(lanes == 0, query_squares, key_squares)
-    ss_copies = share_squares(0, squares)
+    more, key_squares = share_squares(1, acc_b[...])
+    ss_copies += more
     inverse = total_squares(0, squares)
     for g in range(groups):
         at = slice(g * padded, (g + 1) * padded)
-        query_scale = inverse[at, 0:1]
         for h in range(heads):
             cols = slice(h * HD, (h + 1) * HD)
-            normed = acc[at, cols] * query_scale * q_gain[:, cols]
+            normed = acc[at, cols] * inverse[at, :] * q_gain[:, cols]
             q_buf[seq, at, cols] = rotate(normed, caches + g, padded).astype(BF16)
 
     def q_copy(source, send, to):
@@ -262,130 +297,152 @@
     q_sends.append(q_copy(seq, q_fwd_sem.at[0], mate_x))
     q_sends[-1].start()
 
+    w_copies[2].wait()
+    project(0, 2, acc)
+    inverse = total_squares(1, key_squares)
     for g in range(groups):
         at = slice(g * padded, (g + 1) * padded)
-        key_scale = inverse[at, 1:2]
         place = slice((caches + g) * frame, (caches + g + 1) * frame)
+        v32[place, :] = acc[at, :][:frame, :]
         for h in range(heads):
             cols = slice(h * HD, (h + 1) * HD)
-            normed = acc_b[at, cols] * key_scale * k_gain[:, cols]
+            normed = acc_b[at, cols] * inverse[at, :] * k_gain[:, cols]
             k32[place, cols] = rotate(normed, caches + g, padded)[:frame, :]
-    w_copies[2].wait()
-    project(0, 2, acc)
-    for g in range(groups):
-        place = slice((caches + g) * frame, (caches + g + 1) * frame)
-        v32[place, :] = acc[g * padded : g * padded + frame, :]
     kb[...] = k32[...].astype(BF16)
     vb[...] = v32[...].astype(BF16)
 
+    in_copies[1].wait()
     forwards += gather_x(1)
     modulate(1, jnp.int32(0))
     project(1, 1, acc_b)
-    squares = jnp.broadcast_to(jnp.sum(acc_b[...] * acc_b[...], axis=-1, keepdims=True), (rows, HD))
-    ss_copies += share_squares(1, squares)
-    project(1, 2, acc)
-
-    scale = HD ** (-0.5)
-    column = lax.broadcasted_iota(jnp.int32, (rows, key_rows), 1)
-
-    def attend(source, part, stat):
-        stats = jnp.zeros((rows, HD), F32)
+    more, clean_squares = share_squares(2, acc_b[...])
+    ss_copies += more
+
+    sharp = HD ** (-0.5) * 1.4426950408889634
+    last = key_rows - HD
+    column = lax.broadcasted_iota(jnp.int32, (NX * rows, HD), 1) + last
+    wide = lax.broadcasted_iota(jnp.int32, (NX * rows, HD), 1)
+
+    def attend(there, slot):
+        stats = jnp.zeros((NX * rows, HD), F32)
+        queries = q_buf[pl.ds(there, NX)].reshape(NX * rows, inner)
         for h in range(heads):
             cols = slice(h * HD, (h + 1) * HD)
             scores = lax.dot_general(
-                q_buf[source, :, cols], kb[:, cols], (((1,), (1,)), ((), ())),
+                queries[:, cols], kb[:, cols], (((1,), (1,)), ((), ())),
                 preferred_element_type=F32,
-            ) * scale
-            scores = jnp.where(column < n_keys, scores, -3.0e38)
+            )
+            edge = jnp.where(column < n_keys, scores[:, last:], -3.0e38)
+            scores = jnp.concatenate([scores[:, :last], edge], axis=1)
             top = jnp.max(scores, axis=-1, keepdims=True)
-            weights = jnp.exp(scores - top)
+            weights = jnp.exp2((scores - top) * sharp)
             total = jnp.sum(weights, axis=-1, keepdims=True)
-            part[:, cols] = jnp.dot(
-                weights.astype(BF16), vb[:, cols], preferred_element_type=F32
-            ).astype(BF16)
-            stats = jnp.where(lanes == h, top, stats)
-            stats = jnp.where(lanes == half + h, total, stats)
-        stat[...] = stats
-
-    def part_copy(slot, to):
+            sums = jnp.dot(weights.astype(BF16), vb[:, cols], preferred_element_type=F32)
+            own_part[slot, :, :, cols] = sums.reshape(NX, rows, HD)
+            stats = jnp.where(wide == h, top, stats)
+            stats = jnp.where(wide == 8 + h, total, stats)
+        own_stat[slot] = stats.reshape(NX, rows, HD)
+
+    def mate_copy(step):
         return (
             remote(
-                part_send.at[to], part_recv.at[slot], p_send_sem.at[to], p_recv_sem.at[slot],
-                "seq", to,
+                part_mate.at[step], mate_in.at[step], m_send_sem.at[step], m_recv_sem.at[step],
+                "seq", mate_x,
             ),
             remote(
-                stat_send.at[to], stat_recv.at[slot], t_send_sem.at[to], t_recv_sem.at[slot],
-                "seq", to,
+                stat_mate.at[step], mate_stat.at[step], mt_send_sem.at[step],
+                mt_recv_sem.at[step], "seq", mate_x,
             ),
         )
 
-    @pl.loop(0, n_seq)
+    def part_copy(from_z, to_z):
+        to = to_z * NX + x
+        return (
+            remote(
+                part_send.at[to_z], part_recv.at[from_z], p_send_sem.at[to_z],
+                p_recv_sem.at[from_z], "seq", to,
+            ),
+            remote(
+                stat_send.at[to_z], stat_recv.at[from_z], t_send_sem.at[to_z],
+                t_recv_sem.at[from_z], "seq", to,
+            ),
+        )
+
+    @pl.loop(0, n_z + 1)
+    def _(step):
+        @pl.when(step < n_z)
+        def _():
+            there = lax.rem(z + n_z - step, n_z) * NX
+
+            @pl.when(step > 0)
+            def _():
+                q_copy(there + x, q_send_sem.at[0], mate_x).wait_recv()
+                q_copy(there + x, q_fwd_sem.at[step], mate_x).start()
+
+            q_copy(there + (1 - x), q_send_sem.at[0], mate_x).wait_recv()
+            slot = lax.rem(step, 2)
+            attend(there, slot)
+            part_mate[step] = own_part[slot, 1 - x].astype(BF16)
+            stat_mate[step] = to_link(own_stat[slot, 1 - x])
+            for copy in mate_copy(step):
+                copy.start()
+
+        @pl.when(step > 0)
+        def _():
+            done = step - 1
+            slot = lax.rem(done, 2)
+            to_z = lax.rem(z + n_z - done, n_z)
+            for copy in mate_copy(done):
+                copy.wait_recv()
+            mine = own_stat[slot, x]
+            other = from_link(mate_stat[done])
+            top = jnp.maximum(mine, other)
+            weight = jnp.exp2((mine - top) * sharp)
+            weight_other = jnp.exp2((other - top) * sharp)
+            total = weight * pltpu.roll(mine, HD - 8, 1) + weight_other * pltpu.roll(other, HD - 8, 1)
+            stats = jnp.where(lanes < 8, top, pltpu.roll(total, 8, 1))
+            for h in range(heads):
+                cols = slice(h * HD, (h + 1) * HD)
+                part_send[to_z, :, cols] = (
+                    own_part[slot, x, :, cols] * weight[:, h : h + 1]
+                    + mate_in[done, :, cols].astype(F32) * weight_other[:, h : h + 1]
+                ).astype(BF16)
+            stat_send[to_z] = to_link(stats)
+
+            @pl.when(done > 0)
+            def _():
+                for copy in part_copy(z, to_z):
+                    copy.start()
+
+    part_recv[z] = part_send[z]
+    stat_recv[z] = stat_send[z]
+
+    project(1, 2, acc)
+    inverse = total_squares(2, clean_squares)
+    for g in range(groups):
+        at = slice(g * padded, (g + 1) * padded)
+        normed = acc_b[at, :] * inverse[at, :] * k_gain[...]
+        fresh_keys[g] = normed[:frame, :].astype(BF16)
+        fresh_values[g] = acc[at, :][:frame, :].astype(BF16)
+
+    @pl.loop(1, n_z)
     def _(c):
-        step = c // NX
-        across = c % NX
-        there = lax.rem(z + n_z - step, n_z) * NX
-        source = there + lax.rem(x + across, NX)
-
-        @pl.when(c > 0)
-        def _():
-            q_copy(source, q_send_sem.at[0], mate_x).wait_recv()
-
-        @pl.when((c > 0) & (across == 0))
-        def _():
-            q_copy(source, q_fwd_sem.at[step], mate_x).start()
-
-        attend(source, part_send.at[source], stat_send.at[source])
-
-        @pl.when(c > 0)
-        def _():
-            for copy in part_copy(seq, source):
-                copy.start()
-
-    part_recv[seq] = part_send[seq]
-    stat_recv[seq] = stat_send[seq]
-
-    inverse = total_squares(1, squares)
-    rolling = caches - controls[2]
-    targets = [controls[2] + lax.rem(controls[1] + g, rolling) for g in range(groups)]
-    for h in range(heads):
-        cols = slice(h * HD, (h + 1) * HD)
-        fresh = []
-        for g in range(groups):
-            at = slice(g * padded, (g + 1) * padded)
-            normed = acc_b[at, cols] * inverse[at, 0:1] * k_gain[:, cols]
-            fresh.append(
-                (normed[:frame, :].astype(BF16), acc[at, cols][:frame, :].astype(BF16))
-            )
-        for f in range(caches):
-            keys = cache_keys[f, :, cols]
-            values = cache_values[f, :, cols]
-            for g in range(groups):
-                keys = jnp.where(targets[g] == f, fresh[g][0], keys)
-                values = jnp.where(targets[g] == f, fresh[g][1], values)
-            new_keys[f, :, cols] = keys
-            new_values[f, :, cols] = values
-
-    @pl.loop(1, n_seq)
-    def _(c):
-        source = lax.rem(seq + c, n_seq)
+        source = lax.rem(z + c, n_z)
         for copy in part_copy(source, source):
             copy.wait_recv()
 
-    def highest(j, top):
-        return jnp.maximum(top, stat_recv[j])
-
-    top = lax.fori_loop(1, n_seq, highest, stat_recv[0])
-
-    def summed(j, total):
-        stat = stat_recv[j]
-        weight = jnp.exp(stat - top)
+    stats = [from_link(stat_recv[j]) for j in range(n_z)]
+    top = stats[0]
+    for stat in stats[1:]:
+        top = jnp.maximum(top, stat)
+    total = jnp.zeros((rows, HD), F32)
+    acc[...] = jnp.zeros_like(acc)
+    for j in range(n_z):
+        weight = jnp.exp2((stats[j] - top) * sharp)
+        total = total + weight * pltpu.roll(stats[j], HD - 8, 1)
         for h in range(heads):
             cols = slice(h * HD, (h + 1) * HD)
             acc[:, cols] += part_recv[j, :, cols].astype(F32) * weight[:, h : h + 1]
-        return total + weight * pltpu.roll(stat, half, 1)
-
-    acc[...] = jnp.zeros_like(acc)
-    total = lax.fori_loop(0, n_seq, summed, jnp.zeros((rows, HD), F32))
     for h in range(heads):
         cols = slice(h * HD, (h + 1) * HD)
         result = (acc[:, cols] / total[:, h : h + 1]).astype(BF16)
@@ -400,11 +457,28 @@
         source = lax.rem(z + n_z - step, n_z) * NX + x
         q_copy(source, q_fwd_sem.at[step], mate_x).wait_send()
 
-    @pl.loop(1, n_seq)
+    @pl.loop(1, n_z)
     def _(c):
-        source = lax.rem(seq + c, n_seq)
-        for copy in part_copy(seq, source):
+        to_z = lax.rem(z + c, n_z)
+        for copy in part_copy(z, to_z):
             copy.wait_send()
+
+    @pl.loop(0, n_z)
+    def _(step):
+        for copy in mate_copy(step):
+            copy.wait_send()
+
+
+def write_kernel(controls, keys, values, fresh_keys, fresh_values, new_keys, new_values):
+    caches, groups = keys.shape[0], fresh_keys.shape[0]
+    rolling = caches - controls[2]
+    targets = [controls[2] + lax.rem(controls[1] + g, rolling) for g in range(groups)]
+    for old, fresh, new in ((keys, fresh_keys, new_keys), (values, fresh_values, new_values)):
+        for f in range(caches):
+            kept = old[f]
+            for g in range(groups):
+                kept = jnp.where(targets[g] == f, fresh[g], kept)
+            new[f] = kept
 
 
 def body(n_seq, n_head, hidden, clean, w_query, w_key, w_value, q_gain, k_gain, keys, values,
@@ -425,17 +499,19 @@
     smem = pl.BlockSpec(memory_space=pltpu.SMEM)
     hbm = pl.BlockSpec(memory_space=pl.ANY)
     dma = pltpu.SemaphoreType.DMA
-    return pl.pallas_call(
+    n_z = n_seq // NX
+    link_rows = -(-rows // 128) * 128
+    fresh = jax.ShapeDtypeStruct((groups, frame, inner), BF16)
+    out, fresh_keys, fresh_values = pl.pallas_call(
         functools.partial(kernel, n_seq, n_head),
-        out_shape=(
-            jax.ShapeDtypeStruct((groups, frame, inner), BF16),
-            jax.ShapeDtypeStruct(keys.shape, BF16),
-            jax.ShapeDtypeStruct(values.shape, BF16),
-        ),
-        in_specs=[vmem, vmem, hbm, hbm, hbm, vmem, vmem, vmem, vmem, vmem, vmem, smem, smem],
+        out_shape=(fresh, fresh, fresh),
+        in_specs=[hbm, hbm, hbm, hbm, hbm, vmem, vmem, hbm, hbm, hbm, vmem, smem, smem],
         out_specs=(vmem, vmem, vmem),
         scratch_shapes=[
             pltpu.VMEM((3,) + w_query.shape, BF16),
+            pltpu.VMEM(modulation.shape, F32),
+            pltpu.VMEM(keys.shape, BF16),
+            pltpu.VMEM(values.shape, BF16),
             pltpu.VMEM((2, n_head, groups, frame, shard), BF16),
             pltpu.VMEM((2, n_head, rows, shard), BF16),
             pltpu.VMEM((rows, inner), F32),
@@ -446,25 +522,36 @@
             pltpu.VMEM((key_rows, inner), BF16),
             pltpu.VMEM((key_rows, inner), BF16),
             pltpu.VMEM((n_seq, rows, inner), BF16),
-            pltpu.VMEM((n_seq, rows, inner), BF16),
-            pltpu.VMEM((n_seq, rows, inner), BF16),
-            pltpu.VMEM((n_seq, rows, HD), F32),
-            pltpu.VMEM((n_seq, rows, HD), F32),
-            pltpu.VMEM((2, rows, HD), F32),
-            pltpu.VMEM((2, n_head, rows, HD), F32),
+            pltpu.VMEM((n_z, rows, inner), BF16),
+            pltpu.VMEM((n_z, rows, inner), BF16),
+            pltpu.VMEM((n_z, 16, link_rows), F32),
+            pltpu.VMEM((n_z, 16, link_rows), F32),
+            pltpu.VMEM((3, 16, link_rows), F32),
+            pltpu.VMEM((3, n_head, 16, link_rows), F32),
+            pltpu.VMEM((2, NX, rows, inner), F32),
+            pltpu.VMEM((2, NX, rows, HD), F32),
+            pltpu.VMEM((n_z, rows, inner), BF16),
+            pltpu.VMEM((n_z, 16, link_rows), F32),
+            pltpu.VMEM((n_z, rows, inner), BF16),
+            pltpu.VMEM((n_z, 16, link_rows), F32),
             dma((3,)),
+            dma((5,)),
             dma((2, n_head)),
             dma((2, n_head)),
             dma((2, n_head)),
-            dma((2, n_head)),
-            dma((2, n_head)),
+            dma((3, n_head)),
+            dma((3, n_head)),
             dma((n_seq,)),
             dma((n_seq,)),
             dma((n_seq,)),
-            dma((n_seq,)),
-            dma((n_seq,)),
-            dma((n_seq,)),
-            dma((n_seq,)),
+            dma((n_z,)),
+            dma((n_z,)),
+            dma((n_z,)),
+            dma((n_z,)),
+            dma((n_z,)),
+            dma((n_z,)),
+            dma((n_z,)),
+            dma((n_z,)),
         ],
         compiler_params=pltpu.CompilerParams(
             collective_id=0, has_side_effects=True, vmem_limit_bytes=60 * 1024 * 1024
@@ -472,6 +559,17 @@
         name="block",
     )(hidden, clean, w_query, w_key, w_value, q_gain[None, :], k_gain[None, :], keys, values,
       modulation, frequency, controls, frame_pos)
+    new_keys, new_values = pl.pallas_call(
+        write_kernel,
+        out_shape=(
+            jax.ShapeDtypeStruct(keys.shape, BF16),
+            jax.ShapeDtypeStruct(values.shape, BF16),
+        ),
+        in_specs=[smem, vmem, vmem, vmem, vmem],
+        out_specs=(vmem, vmem),
+        name="write",
+    )(controls, keys, values, fresh_keys, fresh_values)
+    return out, new_keys, new_values
 
 
 def solution(mesh):

time: 87.7 us -> 76.5 us (0.87)
  Pallas kernels: 75.4 us -> 68.1 us
  local copies, waits for them, and re-layouts: 11.3 us -> 7.49 us
    pallas_call x1 -> x2, Pallas kernels: 75.4 us -> 68.1 us  [the longest x1 65.7 us: body(): pl.pallas_call(functools.partial(kernel, n_seq, n_head), out_shape=(fresh...]
    unnamed x4 -> x3, local copies, waits for them, and re-layouts: 7.11 us -> 4.94 us
    pallas_call x1 -> x0, local copies, waits for them, and re-layouts: 1.63 us -> none  [body(): pl.pallas_call(functools.partial(kernel, n_seq, n_head), out_shape=(jax.S...]
where the time goes in v2:
time: 76.5 us; the launch traced here: 76.2 us
  Pallas kernels  68.1 us (89%)
  local copies, waits for them, and re-layouts  7.49 us (10%)
    pallas_call x1, Pallas kernels, body(): pl.pallas_call(functools.partial(kernel, n_seq, n_head), out_shape=(fresh...  65.7 us
    unnamed x3, local copies, waits for them, and re-layouts  4.94 us
    pallas_call x1, Pallas kernels, body(): pl.pallas_call(write_kernel, out_shape=(jax.ShapeDtypeStruct(keys.shape,...  2.34 us

profile of v2, /device:TPU:0, one launch (start us, length us, event | category | flops | bytes accessed | tf_op | source)
XLA Modules:
  0.0 76.2 jit_solution(13070804765889287807)
XLA Ops:
  0.6 1.3 %broadcast_in_dim.6.q_gain = f32[1,640]{1,0:T(1,128)} reshape(f32[640]{0:T(1024)} %param.18) | data formatting | bytes 5120 | tf_op jit(solution)/shard_map/broadcast_in_dim | solution.py:560
  1.9 1.3 %broadcast_in_dim.7.k_gain = f32[1,640]{1,0:T(1,128)} reshape(f32[640]{0:T(1024)} %param.19) | data formatting | bytes 5120 | tf_op jit(solution)/shard_map/broadcast_in_dim | solution.py:560
  3.2 1.7 %copy.16.x_noisy = bf16[2,44,1280]{2,1,0:T(8,128)(2,1)} copy(bf16[2,44,1280]{2,0,1:T(2,128)(2,1)} %param.13) | data formatting | bytes 450560 | tf_op args[0]
  4.8 1.7 %copy.17.x_clean = bf16[2,44,1280]{2,1,0:T(8,128)(2,1)} copy(bf16[2,44,1280]{2,0,1:T(2,128)(2,1)} %param.14) | data formatting | bytes 450560 | tf_op args[1]
  6.5 65.7 %block.1 = (bf16[2,44,640]{2,1,0:T(8,128)(2,1)}, bf16[2,44,640]{2,1,0:T(8,128)(2,1)}, bf16[2,44,640]{2,1,0:T(8,128)(2,1)}) custom-call(bf16[2,44,1280]{2,1,0:T(8,128)(2,1)} %copy.16.x_noisy, bf16[2,44,1280]{2,1,0:T(8,128)(2,1)} %copy.17.x_clean, bf16[5120,640]{1,0:T(8,128)(2,1)} %w_query.1, bf16[5120,640]{1,0:T(8,128)(2,1)} %w_key.1, ...), custom_call_target="tpu_custom_call" | custom-call | tf_op jit(solution)/shard_map/block/pallas_call | solution.py:505
  72.2 1.6 %copy.18 = bf16[2,44,640]{2,0,1:T(2,128)(2,1)} copy(bf16[2,44,640]{2,1,0:T(8,128)(2,1)} %get-tuple-element.13) | data formatting | bytes 225280
  73.8 2.3 %write.1 = (bf16[9,44,640]{2,1,0:T(8,128)(2,1)}, bf16[9,44,640]{2,1,0:T(8,128)(2,1)}) custom-call(s32[3]{0:T(128)} %controls.3, bf16[9,44,640]{2,1,0:T(8,128)(2,1)} %keys.1, bf16[9,44,640]{2,1,0:T(8,128)(2,1)} %values.1, bf16[2,44,640]{2,1,0:T(8,128)(2,1)} %get-tuple-element.9.fresh_keys, bf16[2,44,640]{2,1,0:T(8,128)(2,1)} %get-tuple-element.10.fresh_values), custom_call_target="tpu_custom_call" | custom-call | tf_op jit(solution)/shard_map/write/pallas_call | solution.py:562

commit v3 on v2

--- a/solution.py
+++ b/solution.py
@@ -101,6 +101,18 @@
     yy = head // 2
     mate = yy * 2 + (1 - core)
 
+    def partner(step):
+        if n_z & (n_z - 1):
+            return lax.rem(z + step, n_z)
+        other, bit = 0, 1
+        while bit < n_z:
+            other = other + (z // bit + step // bit) % 2 * bit
+            bit *= 2
+        return other
+
+    def source_z(step):
+        return lax.rem(z + n_z - step, n_z) if n_z & (n_z - 1) else partner(step)
+
     barrier = pltpu.get_barrier_semaphore()
     for step in range(1, n_head):
         pl.semaphore_signal(
@@ -146,7 +158,8 @@
             x_sends.append(x_copy(kind, own_x[kind], head, x_send_sem.at[kind, step], to))
             x_sends[-1].start()
         x_sends.append(x_copy(kind, own_x[kind], head, x_send_sem.at[kind, 0], mate))
-        x_sends[-1].start()
+        if kind == 0:
+            x_sends[-1].start()
 
     y[...] = jnp.zeros_like(y)
     k32[n_keys:, :] = jnp.zeros((key_rows - n_keys, inner), F32)
@@ -194,6 +207,8 @@
                 x_copy(kind, xg.at[kind, source], source, x_fwd_sem.at[kind, step], mate)
             )
             forwards[-1].start()
+        if kind == 0:
+            x_sends[-1].start()
         for step in range(n_y):
             source = lax.rem(yy + n_y - step, n_y) * 2 + (1 - core)
             x_copy(kind, own_x[kind], source, x_send_sem.at[kind, 0], mate).wait_recv()
@@ -284,7 +299,7 @@
         at = slice(g * padded, (g + 1) * padded)
         for h in range(heads):
             cols = slice(h * HD, (h + 1) * HD)
-            normed = acc[at, cols] * inverse[at, :] * q_gain[:, cols]
+            normed = acc[at, cols] * inverse[at, :] * q_gain[cols][None, :]
             q_buf[seq, at, cols] = rotate(normed, caches + g, padded).astype(BF16)
 
     def q_copy(source, send, to):
@@ -292,7 +307,7 @@
 
     q_sends = []
     for step in range(1, n_z):
-        q_sends.append(q_copy(seq, q_send_sem.at[step], lax.rem(z + step, n_z) * NX + x))
+        q_sends.append(q_copy(seq, q_send_sem.at[step], partner(step) * NX + x))
         q_sends[-1].start()
     q_sends.append(q_copy(seq, q_fwd_sem.at[0], mate_x))
     q_sends[-1].start()
@@ -306,14 +321,21 @@
         v32[place, :] = acc[at, :][:frame, :]
         for h in range(heads):
             cols = slice(h * HD, (h + 1) * HD)
-            normed = acc_b[at, cols] * inverse[at, :] * k_gain[:, cols]
+            normed = acc_b[at, cols] * inverse[at, :] * k_gain[cols][None, :]
             k32[place, cols] = rotate(normed, caches + g, padded)[:frame, :]
     kb[...] = k32[...].astype(BF16)
     vb[...] = v32[...].astype(BF16)
 
+    def pass_on(step):
+        source = source_z(step) * NX + x
+        q_copy(source, q_send_sem.at[0], mate_x).wait_recv()
+        q_copy(source, q_fwd_sem.at[step], mate_x).start()
+
     in_copies[1].wait()
     forwards += gather_x(1)
     modulate(1, jnp.int32(0))
+    if n_z > 1:
+        pass_on(1)
     project(1, 1, acc_b)
     more, clean_squares = share_squares(2, acc_b[...])
     ss_copies += more
@@ -368,62 +390,63 @@
             ),
         )
 
-    @pl.loop(0, n_z + 1)
+    def merge(done):
+        slot = lax.rem(done, 2)
+        to_z = source_z(done)
+        for copy in mate_copy(done):
+            copy.wait_recv()
+        mine = own_stat[slot, x]
+        other = from_link(mate_stat[done])
+        top = jnp.maximum(mine, other)
+        weight = jnp.exp2((mine - top) * sharp)
+        weight_other = jnp.exp2((other - top) * sharp)
+        total = weight * pltpu.roll(mine, HD - 8, 1) + weight_other * pltpu.roll(other, HD - 8, 1)
+        for h in range(heads):
+            cols = slice(h * HD, (h + 1) * HD)
+            part_send[to_z, :, cols] = (
+                own_part[slot, x, :, cols] * weight[:, h : h + 1]
+                + mate_in[done, :, cols].astype(F32) * weight_other[:, h : h + 1]
+            ).astype(BF16)
+        stat_send[to_z] = to_link(jnp.where(lanes < 8, top, pltpu.roll(total, 8, 1)))
+
+    @pl.loop(0, n_z)
     def _(step):
-        @pl.when(step < n_z)
+        there = source_z(step) * NX
+        q_copy(there + (1 - x), q_send_sem.at[0], mate_x).wait_recv()
+        slot = lax.rem(step, 2)
+        attend(there, slot)
+        part_mate[step] = own_part[slot, 1 - x].astype(BF16)
+        stat_mate[step] = to_link(own_stat[slot, 1 - x])
+        for copy in mate_copy(step):
+            copy.start()
+
+        @pl.when(step + 2 < n_z)
         def _():
-            there = lax.rem(z + n_z - step, n_z) * NX
-
-            @pl.when(step > 0)
-            def _():
-                q_copy(there + x, q_send_sem.at[0], mate_x).wait_recv()
-                q_copy(there + x, q_fwd_sem.at[step], mate_x).start()
-
-            q_copy(there + (1 - x), q_send_sem.at[0], mate_x).wait_recv()
-            slot = lax.rem(step, 2)
-            attend(there, slot)
-            part_mate[step] = own_part[slot, 1 - x].astype(BF16)
-            stat_mate[step] = to_link(own_stat[slot, 1 - x])
-            for copy in mate_copy(step):
-                copy.start()
+            pass_on(step + 2)
 
         @pl.when(step > 0)
         def _():
-            done = step - 1
-            slot = lax.rem(done, 2)
-            to_z = lax.rem(z + n_z - done, n_z)
-            for copy in mate_copy(done):
-                copy.wait_recv()
-            mine = own_stat[slot, x]
-            other = from_link(mate_stat[done])
-            top = jnp.maximum(mine, other)
-            weight = jnp.exp2((mine - top) * sharp)
-            weight_other = jnp.exp2((other - top) * sharp)
-            total = weight * pltpu.roll(mine, HD - 8, 1) + weight_other * pltpu.roll(other, HD - 8, 1)
-            stats = jnp.where(lanes < 8, top, pltpu.roll(total, 8, 1))
-            for h in range(heads):
-                cols = slice(h * HD, (h + 1) * HD)
-                part_send[to_z, :, cols] = (
-                    own_part[slot, x, :, cols] * weight[:, h : h + 1]
-                    + mate_in[done, :, cols].astype(F32) * weight_other[:, h : h + 1]
-                ).astype(BF16)
-            stat_send[to_z] = to_link(stats)
-
-            @pl.when(done > 0)
+            merge(step - 1)
+
+            @pl.when(step > 1)
             def _():
-                for copy in part_copy(z, to_z):
+                for copy in part_copy(z, source_z(step - 1)):
                     copy.start()
-
-    part_recv[z] = part_send[z]
-    stat_recv[z] = stat_send[z]
 
     project(1, 2, acc)
     inverse = total_squares(2, clean_squares)
     for g in range(groups):
         at = slice(g * padded, (g + 1) * padded)
-        normed = acc_b[at, :] * inverse[at, :] * k_gain[...]
+        normed = acc_b[at, :] * inverse[at, :] * k_gain[...][None, :]
         fresh_keys[g] = normed[:frame, :].astype(BF16)
         fresh_values[g] = acc[at, :][:frame, :].astype(BF16)
+
+    merge(n_z - 1)
+    if n_z > 1:
+        for copy in part_copy(z, source_z(n_z - 1)):
+            copy.start()
+    part_recv[z] = part_send[z]
+    stat_recv[z] = stat_send[z]
 
     @pl.loop(1, n_z)
     def _(c):
@@ -454,8 +477,7 @@
 
     @pl.loop(1, n_z)
     def _(step):
-        source = lax.rem(z + n_z - step, n_z) * NX + x
-        q_copy(source, q_fwd_sem.at[step], mate_x).wait_send()
+        q_copy(source_z(step) * NX + x, q_fwd_sem.at[step], mate_x).wait_send()
 
     @pl.loop(1, n_z)
     def _(c):
@@ -557,7 +579,7 @@
             collective_id=0, has_side_effects=True, vmem_limit_bytes=60 * 1024 * 1024
         ),
         name="block",
-    )(hidden, clean, w_query, w_key, w_value, q_gain[None, :], k_gain[None, :], keys, values,
+    )(hidden, clean, w_query, w_key, w_value, q_gain, k_gain, keys, values,
       modulation, frequency, controls, frame_pos)
     new_keys, new_values = pl.pallas_call(
         write_kernel,

time: 76.5 us -> 66.7 us (0.87)
  Pallas kernels: 68.1 us -> 60.8 us
  local copies, waits for them, and re-layouts: 7.49 us -> 4.95 us
    pallas_call x1, Pallas kernels: 65.7 us -> 58.5 us  [body(): pl.pallas_call(functools.partial(kernel, n_seq, n_head), out_shape=(fresh...]
    broadcast_in_dim x2 -> x0, local copies, waits for them, and re-layouts: 2.55 us -> none  [the longest x1 1.28 us: body(): k_gain[None, :]]
where the time goes in v3:
time: 66.7 us; the launch traced here: 66.4 us
  Pallas kernels  60.8 us (91%)
  local copies, waits for them, and re-layouts  4.95 us (7%)
    pallas_call x1, Pallas kernels, body(): pl.pallas_call(functools.partial(kernel, n_seq, n_head), out_shape=(fresh...  58.5 us
    unnamed x3, local copies, waits for them, and re-layouts  4.95 us
    pallas_call x1, Pallas kernels, body(): pl.pallas_call(write_kernel, out_shape=(jax.ShapeDtypeStruct(keys.shape,...  2.34 us

profile of v3, /device:TPU:0, one launch (start us, length us, event | category | flops | bytes accessed | tf_op | source)
XLA Modules:
  0.0 66.4 jit_solution(429232202947774673)
XLA Ops:
  0.6 1.7 %copy.16.x_noisy = bf16[2,44,1280]{2,1,0:T(8,128)(2,1)} copy(bf16[2,44,1280]{2,0,1:T(2,128)(2,1)} %param.13) | data formatting | bytes 450560 | tf_op args[0]
  2.3 1.7 %copy.17.x_clean = bf16[2,44,1280]{2,1,0:T(8,128)(2,1)} copy(bf16[2,44,1280]{2,0,1:T(2,128)(2,1)} %param.14) | data formatting | bytes 450560 | tf_op args[1]
  3.9 58.5 %block.1 = (bf16[2,44,640]{2,1,0:T(8,128)(2,1)}, bf16[2,44,640]{2,1,0:T(8,128)(2,1)}, bf16[2,44,640]{2,1,0:T(8,128)(2,1)}) custom-call(bf16[2,44,1280]{2,1,0:T(8,128)(2,1)} %copy.16.x_noisy, bf16[2,44,1280]{2,1,0:T(8,128)(2,1)} %copy.17.x_clean, bf16[5120,640]{1,0:T(8,128)(2,1)} %w_query.1, bf16[5120,640]{1,0:T(8,128)(2,1)} %w_key.1, ...), custom_call_target="tpu_custom_call" | custom-call | tf_op jit(solution)/shard_map/block/pallas_call | solution.py:527
  62.5 1.6 %copy.18 = bf16[2,44,640]{2,0,1:T(2,128)(2,1)} copy(bf16[2,44,640]{2,1,0:T(8,128)(2,1)} %get-tuple-element.13) | data formatting | bytes 225280
  64.1 2.3 %write.1 = (bf16[9,44,640]{2,1,0:T(8,128)(2,1)}, bf16[9,44,640]{2,1,0:T(8,128)(2,1)}) custom-call(s32[3]{0:T(128)} %controls.3, bf16[9,44,640]{2,1,0:T(8,128)(2,1)} %keys.1, bf16[9,44,640]{2,1,0:T(8,128)(2,1)} %values.1, bf16[2,44,640]{2,1,0:T(8,128)(2,1)} %get-tuple-element.9.fresh_keys, bf16[2,44,640]{2,1,0:T(8,128)(2,1)} %get-tuple-element.10.fresh_values), custom_call_target="tpu_custom_call" | custom-call | tf_op jit(solution)/shard_map/write/pallas_call | solution.py:584

commit v4 on v3

--- a/solution.py
+++ b/solution.py
@@ -508,7 +508,7 @@
     groups, frame, shard = hidden.shape
     caches = keys.shape[0]
     inner = w_query.shape[1]
-    padded = -(-frame // 16) * 16
+    padded = frame
     rows = groups * padded
     key_rows = -(-((caches + groups) * frame) // 128) * 128
     half = HD // 2

time: 66.7 us -> 65 us (0.975)
  Pallas kernels: 60.8 us -> 59.2 us
    pallas_call x1, Pallas kernels: 58.5 us -> 56.9 us  [body(): pl.pallas_call(functools.partial(kernel, n_seq, n_head), out_shape=(fresh...]
where the time goes in v4:
time: 65 us; the launch traced here: 64.8 us
  Pallas kernels  59.2 us (91%)
  local copies, waits for them, and re-layouts  4.95 us (8%)
    pallas_call x1, Pallas kernels, body(): pl.pallas_call(functools.partial(kernel, n_seq, n_head), out_shape=(fresh...  56.9 us
    unnamed x3, local copies, waits for them, and re-layouts  4.95 us
    pallas_call x1, Pallas kernels, body(): pl.pallas_call(write_kernel, out_shape=(jax.ShapeDtypeStruct(keys.shape,...  2.34 us

profile of v4, /device:TPU:0, one launch (start us, length us, event | category | flops | bytes accessed | tf_op | source)
XLA Modules:
  0.0 64.8 jit_solution(7393887995220939997)
XLA Ops:
  0.6 1.7 %copy.16.x_noisy = bf16[2,44,1280]{2,1,0:T(8,128)(2,1)} copy(bf16[2,44,1280]{2,0,1:T(2,128)(2,1)} %param.13) | data formatting | bytes 450560 | tf_op args[0]
  2.3 1.7 %copy.17.x_clean = bf16[2,44,1280]{2,1,0:T(8,128)(2,1)} copy(bf16[2,44,1280]{2,0,1:T(2,128)(2,1)} %param.14) | data formatting | bytes 450560 | tf_op args[1]
  3.9 56.9 %block.1 = (bf16[2,44,640]{2,1,0:T(8,128)(2,1)}, bf16[2,44,640]{2,1,0:T(8,128)(2,1)}, bf16[2,44,640]{2,1,0:T(8,128)(2,1)}) custom-call(bf16[2,44,1280]{2,1,0:T(8,128)(2,1)} %copy.16.x_noisy, bf16[2,44,1280]{2,1,0:T(8,128)(2,1)} %copy.17.x_clean, bf16[5120,640]{1,0:T(8,128)(2,1)} %w_query.1, bf16[5120,640]{1,0:T(8,128)(2,1)} %w_key.1, ...), custom_call_target="tpu_custom_call" | custom-call | tf_op jit(solution)/shard_map/block/pallas_call | solution.py:527
  60.8 1.6 %copy.18 = bf16[2,44,640]{2,0,1:T(2,128)(2,1)} copy(bf16[2,44,640]{2,1,0:T(8,128)(2,1)} %get-tuple-element.13) | data formatting | bytes 225280
  62.4 2.3 %write.1 = (bf16[9,44,640]{2,1,0:T(8,128)(2,1)}, bf16[9,44,640]{2,1,0:T(8,128)(2,1)}) custom-call(s32[3]{0:T(128)} %controls.3, bf16[9,44,640]{2,1,0:T(8,128)(2,1)} %keys.1, bf16[9,44,640]{2,1,0:T(8,128)(2,1)} %values.1, bf16[2,44,640]{2,1,0:T(8,128)(2,1)} %get-tuple-element.9.fresh_keys, bf16[2,44,640]{2,1,0:T(8,128)(2,1)} %get-tuple-element.10.fresh_values), custom_call_target="tpu_custom_call" | custom-call | tf_op jit(solution)/shard_map/write/pallas_call | solution.py:584
